TPU v7x, 256 devices: a whole 4x4x8 slice. The times are simulated.
256 devices in a mesh: leaf: 8 (over y, core), node: 32 (over z, x).
Axes of the slice: x: 4, y: 4, z: 8, core: 2. Of those that a mesh axis runs over, the one named last changes fastest.
Arguments:
- sources: bfloat16 [2048, 131072], P('node', 'leaf'), may hold values from -6 to 6
- block_inverse: bfloat16 [512, 131072], P(None, ('leaf', 'node')), may hold values from -0.25 to 0.25
- basis_left: bfloat16 [64, 131072], P(None, ('leaf', 'node')), may hold values from -0.046875 to 0.046875
- basis_right: bfloat16 [64, 131072], P(None, ('leaf', 'node')), may hold values from -0.75 to 0.75
- couple_in: bfloat16 [64, 131072], P(None, ('leaf', 'node')), may hold values from -0.046875 to 0.046875
- couple_out: bfloat16 [64, 131072], P(None, ('leaf', 'node')), may hold values from -0.5 to 0.5
- column_of_shot: int32 [2048], replicated, may hold values from 0 to 2047, each once
- cell_map: int32 [131072], P(('leaf', 'node')), may hold values from 0 to 65535
Outputs:
- solution: bfloat16 [2048, 131072], P(None, ('leaf', 'node'))
- gradient: float32 [65536], P('node')
Inputs may be any that keep to these rules, and one draw needn't show every extreme that they name: `column_of_shot`: a permutation of the 2048 column numbers.
All inputs are finite; a program needn't handle non-finite values.
Results may differ from a plain program's by a relative error of at most 0.02.
Values may be sent and summed in bfloat16 or wider, within the bound.
No kernel may reach another device: no remote copies, remote signals or barrier semaphores. Data moves between devices by JAX's collectives and lax.ppermute only.
A program may use at most 64 MiB of HBM per device.

v0:
```python
import functools

import jax
import jax.numpy as jnp
from jax import lax
from jax.experimental import pallas as pl
from jax.experimental.pallas import tpu as pltpu
from jax.sharding import Mesh, PartitionSpec as P

BLOCK = 512
RANK = 64
NZ = 8
NX = 4
NLEAF = 8
LANES = 128
BF = jnp.bfloat16
F32 = jnp.float32
NT = (((1,), (1,)), ((), ()))
VMEM_SPEC = pl.BlockSpec(memory_space=pltpu.VMEM)
SMEM_SPEC = pl.BlockSpec(memory_space=pltpu.SMEM)


def dot(a, b):
    return jnp.dot(a.astype(BF), b.astype(BF), preferred_element_type=F32)


def dot_nt(a, b):
    return lax.dot_general(a.astype(BF), b.astype(BF), NT, preferred_element_type=F32)


def prepare_kernel(d_ref, left_ref, right_ref, cin_ref, cout_ref, w_ref, g_ref, re_ref, lc_ref):
    d = d_ref[...]
    left = left_ref[...]
    right = right_ref[...]
    cin = cin_ref[...]
    both = jnp.concatenate([cout_ref[...], right], axis=0)
    cin_d = dot(cin, d)
    both_dt = dot_nt(both, d)
    w_ref[0:64, :] = left
    w_ref[64:192, :] = both_dt.astype(BF)
    w_ref[192:256, :] = dot_nt(cin_d, d).astype(BF)
    g_ref[:, 0:256] = dot_nt(cin, w_ref[...])
    g_ref[:, 256:384] = dot_nt(right, both)
    re_ref[0:64, :] = right
    re_ref[64:128, :] = (-cin_d).astype(BF)
    lc_ref[0:64, :] = left
    lc_ref[64:128, :] = (-both_dt[0:64, :]).astype(BF)


def prepare(d, left, right, cin, cout):
    return pl.pallas_call(
        prepare_kernel,
        name="prepare",
        out_shape=(
            jax.ShapeDtypeStruct((4 * RANK, BLOCK), BF),
            jax.ShapeDtypeStruct((RANK, 6 * RANK), F32),
            jax.ShapeDtypeStruct((2 * RANK, BLOCK), BF),
            jax.ShapeDtypeStruct((2 * RANK, BLOCK), BF),
        ),
        in_specs=[VMEM_SPEC] * 5,
        out_specs=(VMEM_SPEC,) * 4,
    )(d, left, right, cin, cout)


def project_kernel(x_ref, v_ref, w0, w1, w2, w3, y_ref, p0, p1, p2, p3):
    x = x_ref[0]
    total = None
    for k, w in enumerate((w0, w1, w2, w3)):
        at = pl.multiple_of(lax.rem(x + (NX - k), NX) * BLOCK, BLOCK)
        part = lax.dot_general(v_ref[:, pl.ds(at, BLOCK)], w[...], NT, preferred_element_type=F32)
        total = part if total is None else total + part
    y_ref[...] = total.astype(BF)
    for k, piece in enumerate((p0, p1, p2, p3)):
        at = pl.multiple_of(lax.rem(x + k, NX) * BLOCK, BLOCK)
        piece[...] = v_ref[:, pl.ds(at, BLOCK)]


def project(x, v, ws):
    rows = v.shape[0]
    return pl.pallas_call(
        project_kernel,
        name="project",
        out_shape=(jax.ShapeDtypeStruct((rows, 4 * RANK), BF),)
        + (jax.ShapeDtypeStruct((rows, BLOCK), BF),) * NX,
        in_specs=[SMEM_SPEC] + [VMEM_SPEC] * 5,
        out_specs=(VMEM_SPEC,) * 5,
    )(x, v, *ws)


def recur_kernel(at_ref, y_ref, g_ref, out_ref):
    mine = at_ref[0]
    cols = lambda a, i: a[:, i * RANK : (i + 1) * RANK]
    zero = jnp.zeros((y_ref.shape[1], RANK), F32)
    inc = zero
    held = [zero] * 4
    p_mine = m1_mine = jnp.zeros((RANK, RANK), F32)
    steps, lifts = [], []
    pick = lambda j, new, old: jnp.where(mine == j, new, old)
    for j in range(NLEAF):
        maps = g_ref[at_ref[1 + j]]
        p, s1, s2, s4, m1, m2 = (cols(maps, i) for i in range(6))
        y = y_ref[j].astype(F32)
        proj, y_carry, y_q, y_lift = (cols(y, i) for i in range(4))
        step = -(s1 + dot(p, m1))
        q_map = s2 + dot(p, m2)
        lift_map = s4 + dot_nt(p, s2)
        q = y_q + dot(proj, m2) - dot(inc, q_map)
        lift = y_lift + dot_nt(proj, s2) - dot(inc, lift_map) + dot_nt(q, p)
        held = [pick(j, a, b) for a, b in zip((proj, inc, q, zero), held)]
        p_mine = pick(j, p, p_mine)
        m1_mine = pick(j, m1, m1_mine)
        inc = y_carry + dot(proj, m1) + dot(inc, step)
        steps.append(step)
        lifts.append(lift)
    ret = zero
    ret_mine = zero
    for j in range(NLEAF - 1, -1, -1):
        ret_mine = pick(j, ret, ret_mine)
        if j:
            ret = lifts[j] + dot_nt(ret, steps[j])
    proj, inc, q = held[:3]
    out_ref[:, 0:64] = (proj - dot(inc, p_mine)).astype(BF)
    out_ref[:, 64:128] = inc.astype(BF)
    out_ref[:, 128:192] = (q - dot_nt(ret_mine, m1_mine)).astype(BF)
    out_ref[:, 192:256] = ret_mine.astype(BF)


def recur(at, y, g):
    return pl.pallas_call(
        recur_kernel,
        name="recur",
        out_shape=jax.ShapeDtypeStruct(y.shape[1:], BF),
        in_specs=[SMEM_SPEC, VMEM_SPEC, VMEM_SPEC],
        out_specs=VMEM_SPEC,
    )(at, y, g)


def finish_kernel(x_ref, v0, v1, v2, v3, c_ref, d_ref, re_ref, lc_ref, map_ref, sol_ref, cell_ref):
    x = x_ref[0]
    rows = v0.shape[0]
    corr = jnp.zeros((1, BLOCK), F32)
    for k, v in enumerate((v0, v1, v2, v3)):
        node = lax.rem(x + (NX - k), NX)
        coef = c_ref[:, node].reshape(rows, 4 * RANK)
        fwd = dot(v[...], d_ref[...]) + dot(coef[:, 0:128], re_ref[...])
        fwd = fwd.astype(BF)
        sol = dot_nt(fwd, d_ref[...]) + dot(coef[:, 128:256], lc_ref[...])
        sol = sol.astype(BF)
        sol_ref[pl.ds(k * rows, rows), :] = sol
        corr += jnp.sum(sol.astype(F32) * fwd.astype(F32), axis=0, keepdims=True)
    corr = corr * (1.0 / jnp.sqrt(F32(NX * rows)))
    cell = map_ref[...]
    count = cell_ref.shape[0]
    high = lax.broadcasted_iota(jnp.int32, (count, BLOCK), 0) == cell // LANES
    low = lax.broadcasted_iota(jnp.int32, (LANES, BLOCK), 0) == cell % LANES
    hot = jnp.where(low, 1.0, 0.0).astype(BF)
    first = corr.astype(BF).astype(F32)
    cells = dot_nt(jnp.where(high, first, 0.0), hot) + dot_nt(jnp.where(high, corr - first, 0.0), hot)
    cell_ref[...] = cells.astype(BF)


def finish(x, vs, coef, d, re, lc, cells, cell_rows):
    rows = vs[0].shape[0]
    return pl.pallas_call(
        finish_kernel,
        name="finish",
        out_shape=(
            jax.ShapeDtypeStruct((NX * rows, BLOCK), BF),
            jax.ShapeDtypeStruct((cell_rows, LANES), BF),
        ),
        in_specs=[SMEM_SPEC] + [VMEM_SPEC] * 9,
        out_specs=(VMEM_SPEC,) * 2,
    )(x, *vs, coef, d, re, lc, cells)


def shifted(a, axis, by):
    count = lax.axis_size(axis)
    return lax.ppermute(a, axis, [(i, (i + by) % count) for i in range(count)])


def swapped(a, axis, bit):
    return lax.ppermute(a, axis, [(i, i ^ bit) for i in range(lax.axis_size(axis))])


def broadcast(a, axes):
    count = lax.axis_size(axes)
    return lax.all_to_all(jnp.broadcast_to(a[None], (count, *a.shape)), axes, 0, 0, tiled=True)


def per_device(
    sources, block_inverse, basis_left, basis_right, couple_in, couple_out, column_of_shot, cell_map
):
    node = ("z", "x")
    shots = sources.shape[0]
    z, x, leaf = (lax.axis_index(a) for a in ("z", "x", "leaf"))
    y, core = leaf // 2, leaf % 2
    with jax.named_scope("move_z"):
        by_z = jnp.swapaxes(sources.reshape(shots, NZ, NX * BLOCK), 0, 1)
        v = lax.all_to_all(by_z, "z", 0, 0, tiled=True).reshape(NZ * shots, NX * BLOCK)
    w, g, re, lc = prepare(block_inverse, basis_left, basis_right, couple_in, couple_out)
    with jax.named_scope("maps"):
        ws = [w] + [shifted(w, "x", k) for k in range(1, NX)]
        for axis, bit in (("x", 1), ("x", 2), ("z", 1), ("z", 2), ("z", 4)):
            g = g + swapped(g, axis, bit)
        pair = jnp.stack([g, swapped(g, "leaf", 1)])
        far = [pair] + [shifted(pair, "leaf", 2 * k) for k in range(1, NLEAF // 2)]
        maps = jnp.concatenate(far, axis=0)
    here = x.reshape(1).astype(jnp.int32)
    part, *pieces = project(here, v, ws)
    with jax.named_scope("move_x"):
        vs = [pieces[0]] + [shifted(pieces[k], "x", k) for k in range(1, NX)]
    with jax.named_scope("sum_z"):
        own = lax.all_to_all(part.reshape(NZ, shots, 4 * RANK), "z", 0, 0, tiled=True)
        own = own.astype(F32).sum(axis=0).astype(BF)
    with jax.named_scope("over_leaf"):
        every = broadcast(own, "leaf")
    group = jnp.arange(NLEAF, dtype=jnp.int32)
    place = ((y - group // 2) % (NLEAF // 2)) * 2 + (group % 2 + core) % 2
    at = jnp.concatenate([leaf.reshape(1), place]).astype(jnp.int32)
    coef = recur(at, every, maps)
    with jax.named_scope("over_node"):
        coef = broadcast(coef, node).reshape(NZ, NX, shots, 4 * RANK)
    cell_rows = NZ * NX * 2048 // LANES
    sol, cells = finish(
        here, vs, coef, block_inverse, re, lc, cell_map.reshape(1, BLOCK), cell_rows
    )
    with jax.named_scope("cells"):
        parts = cells.reshape(NZ * NX, cell_rows // (NZ * NX), LANES)
        parts = lax.all_to_all(parts, node, 0, 0, tiled=True)
        slab = parts.astype(F32).sum(axis=0)
        gradient = broadcast(slab, "leaf").sum(axis=0).reshape(-1)
    with jax.named_scope("columns"):
        shot = jnp.arange(NZ * NX * shots, dtype=jnp.int32)
        from_node = shot // shots
        row = ((x - from_node % NX) % NX) * (NZ * shots) + (from_node // NX) * shots + shot % shots
        source_row = jnp.zeros_like(row).at[column_of_shot].set(row)
        solution = jnp.take(sol, source_row, axis=0)
    return solution, gradient


def solution(mesh):
    split = Mesh(mesh.devices.reshape(NLEAF, NZ, NX), ("leaf", "z", "x"))
    block = P(None, ("leaf", "z", "x"))
    return jax.shard_map(
        per_device,
        mesh=split,
        in_specs=(
            P(("z", "x"), "leaf"),
            block,
            block,
            block,
            block,
            block,
            P(),
            P(("leaf", "z", "x")),
        ),
        out_specs=(block, P(("z", "x"))),
        check_vma=False,
    )
```

profile of v0, /device:TPU:1, one launch (start us, length us, event | category | flops | bytes accessed | tf_op | source)
XLA Modules:
  0.0 207.3 jit_solution(1187571767416615837)
XLA Ops:
  0.6 3.2 %copy.14 = bf16[8,8,8,2048]{3,2,0,1:T(8,128)(2,1)} copy(bf16[8,8,8,2048]{3,2,1,0:T(8,128)(2,1)} %bitcast.22) | data formatting | bytes 4194304 | tf_op jit(solution)/shard_map/move_z/reshape | solution.py:198
  3.8 9.0 %all-to-all-start = ((bf16[8,64,2048]{2,1,0:T(8,128)(2,1)}), bf16[8,64,2048]{2,1,0:T(8,128)(2,1)S(1)}, u32[]{:S(2)}, u32[]{:S(2)}) async-start(bf16[8,64,2048]{2,1,0:T(8,128)(2,1)} %bitcast.20), calls=%async_computation | async-start | bytes 4194304 | tf_op jit(solution)/shard_map/move_z/all_to_all | solution.py:199
  12.8 2.5 %prepare.1 = (bf16[256,512]{1,0:T(8,128)(2,1)}, f32[64,384]{1,0:T(8,128)}, bf16[128,512]{1,0:T(8,128)(2,1)}, bf16[128,512]{1,0:T(8,128)(2,1)}) custom-call(bf16[512,512]{1,0:T(8,128)(2,1)} %d_ref.3, bf16[64,512]{1,0:T(8,128)(2,1)} %left_ref.1, bf16[64,512]{1,0:T(8,128)(2,1)} %right_ref.1, bf16[64,512]{1,0:T(8,128)(2,1)} %cin_ref.1, bf16[64,512]{1,0:T(8,128)(2,1)} %cout_ref.1), custom_call_target="tpu_custom_call" | custom-call | tf_op jit(solution)/shard_map/prepare/pallas_call | solution.py:51
  15.3 1.2 collective-permute-start.6
  16.5 2.8 %collective-permute-done.6 = f32[64,384]{1,0:T(8,128)S(1)} collective-permute-done((f32[64,384]{1,0:T(8,128)}, f32[64,384]{1,0:T(8,128)S(1)}, u32[]{:S(2)}, u32[]{:S(2)}) %collective-permute-start.6) | collective-permute-done | bytes 98336 | tf_op jit(solution)/shard_map/maps/ppermute | solution.py:182
  19.3 0.9 add.93
  20.2 2.8 %collective-permute-start.7 = (f32[64,384]{1,0:T(8,128)S(1)}, f32[64,384]{1,0:T(8,128)S(1)}, u32[]{:S(2)}, u32[]{:S(2)}) collective-permute-start(f32[64,384]{1,0:T(8,128)S(1)} %add.93), channel_id=1, source_target_pairs={{0,2},{1,3},{2,0},{3,1},{4,6},{5,7},{6,4},{7,5},{8,10},{9,11},{10,... | collective-permute-start | bytes 294920 | tf_op jit(solution)/shard_map/maps/ppermute | solution.py:182
  23.0 2.5 %collective-permute-done.7 = f32[64,384]{1,0:T(8,128)S(1)} collective-permute-done((f32[64,384]{1,0:T(8,128)S(1)}, f32[64,384]{1,0:T(8,128)S(1)}, u32[]{:S(2)}, u32[]{:S(2)}) %collective-permute-start.7) | collective-permute-done | bytes 98336 | tf_op jit(solution)/shard_map/maps/ppermute | solution.py:182
  25.6 1.6 collective-permute-start.8
  27.1 34.2 %collective-permute-done.8 = f32[64,384]{1,0:T(8,128)S(1)} collective-permute-done((f32[64,384]{1,0:T(8,128)S(1)}, f32[64,384]{1,0:T(8,128)S(1)}, u32[]{:S(2)}, u32[]{:S(2)}) %collective-permute-start.8) | collective-permute-done | bytes 98336 | tf_op jit(solution)/shard_map/maps/ppermute | solution.py:182
  61.4 1.3 collective-permute-start.9
  62.7 1.2 collective-permute-start
  63.9 2.5 %collective-permute-start.1 = (bf16[256,512]{1,0:T(8,128)(2,1)}, bf16[256,512]{1,0:T(8,128)(2,1)}, u32[]{:S(2)}, u32[]{:S(2)}) collective-permute-start(bf16[256,512]{1,0:T(8,128)(2,1)} %get-tuple-element.13.w0), channel_id=1, source_target_pairs={{0,2},{1,3},{2,0},{3,1},{4,6},{5,7},{6,4},{7,5},{8,10},{9,11},{10,... | collective-permute-start | bytes 786440 | tf_op jit(solution)/shard_map/maps/ppermute | solution.py:178
  66.4 1.2 collective-permute-start.2
  67.5 1.9 collective-permute-done.9
  69.4 1.6 collective-permute-start.10
  71.0 5.9 %collective-permute-done.10 = f32[64,384]{1,0:T(8,128)S(1)} collective-permute-done((f32[64,384]{1,0:T(8,128)S(1)}, f32[64,384]{1,0:T(8,128)S(1)}, u32[]{:S(2)}, u32[]{:S(2)}) %collective-permute-start.10) | collective-permute-done | bytes 98336 | tf_op jit(solution)/shard_map/maps/ppermute | solution.py:182
  76.9 3.3 %collective-permute-start.11 = (f32[64,384]{1,0:T(8,128)S(1)}, f32[64,384]{1,0:T(8,128)S(1)}, u32[]{:S(2)}, u32[]{:S(2)}) collective-permute-start(f32[64,384]{1,0:T(8,128)S(1)} %get-tuple-element.25), channel_id=1, source_target_pairs={{0,32},{32,0},{64,96},{96,64},{128,160},{160,128},{192,224},{224,1... | collective-permute-start | bytes 294920 | tf_op jit(solution)/shard_map/maps/ppermute | solution.py:182
  80.2 0.6 pad_add_fusion.at_ref
  80.8 0.0 collective-permute-done.w1
  80.8 0.0 collective-permute-done.1.w2
  80.8 0.0 collective-permute-done.2.w3
  80.8 0.0 all-to-all-done
  80.8 0.0 copy-start
  80.8 0.7 copy-done.7
  81.5 0.7 copy-done
  82.2 3.9 %project.1 = (bf16[512,256]{1,0:T(8,128)(2,1)}, bf16[512,512]{1,0:T(8,128)(2,1)}, bf16[512,512]{1,0:T(8,128)(2,1)}, bf16[512,512]{1,0:T(8,128)(2,1)}, bf16[512,512]{1,0:T(8,128)(2,1)}) custom-call(s32[1]{0:T(128)} %bitcast.x_ref, bf16[512,2048]{1,0:T(8,128)(2,1)} %bitcast.19, bf16[256,512]{1,0:T(8,128)(2,1)} %get-tuple-element.13.w0, ...), custom_call_target="tpu_custom_call" | custom-call | tf_op jit(solution)/shard_map/project/pallas_call | solution.py:80
  86.1 5.9 %all-to-all-start.1 = ((bf16[8,64,256]{2,1,0:T(8,128)(2,1)}), bf16[8,64,256]{2,1,0:T(8,128)(2,1)S(1)}, u32[]{:S(2)}, u32[]{:S(2)}) async-start(bf16[8,64,256]{2,1,0:T(8,128)(2,1)} %bitcast.25), calls=%async_computation.1 | async-start | bytes 524288 | tf_op jit(solution)/shard_map/sum_z/all_to_all | solution.py:213
  92.0 0.0 collective-permute-done.11
  92.0 1.4 collective-permute-start.12
  93.4 2.6 %collective-permute-start.13 = (f32[2,64,384]{2,1,0:T(8,128)S(1)}, f32[2,64,384]{2,1,0:T(8,128)S(1)}, u32[]{:S(2)}, u32[]{:S(2)}) collective-permute-start(f32[2,64,384]{2,1,0:T(8,128)S(1)} %pad_maximum_fusion), channel_id=1, source_target_pairs={{0,128},{32,160},{64,192},{96,224},{128,0},{160,32},{192,64},{224,... | collective-permute-start | bytes 589832 | tf_op jit(solution)/shard_map/maps/ppermute | solution.py:178
  96.0 1.1 collective-permute-start.14
  97.1 2.5 %collective-permute-done.12 = f32[2,64,384]{2,1,0:T(8,128)S(1)} collective-permute-done((f32[2,64,384]{2,1,0:T(8,128)S(1)}, f32[2,64,384]{2,1,0:T(8,128)S(1)}, u32[]{:S(2)}, u32[]{:S(2)}) %collective-permute-start.12) | collective-permute-done | bytes 196640 | tf_op jit(solution)/shard_map/maps/ppermute | solution.py:178
  99.6 4.7 %all-to-all-done.1 = bf16[8,64,256]{2,1,0:T(8,128)(2,1)S(1)} async-done(((bf16[8,64,256]{2,1,0:T(8,128)(2,1)}), bf16[8,64,256]{2,1,0:T(8,128)(2,1)S(1)}, u32[]{:S(2)}, u32[]{:S(2)}) %all-to-all-start.1) | async-done | bytes 262176 | tf_op jit(solution)/shard_map/sum_z/all_to_all | solution.py:213
  104.4 0.7 broadcast_in_dim.35
  105.1 4.9 %all-to-all-start.2 = ((bf16[8,64,256]{2,1,0:T(8,128)(2,1)}), bf16[8,64,256]{2,1,0:T(8,128)(2,1)S(1)}, u32[]{:S(2)}, u32[]{:S(2)}) async-start(bf16[8,64,256]{2,1,0:T(8,128)(2,1)} %broadcast_in_dim.35), calls=%async_computation.2 | async-start | bytes 524288 | tf_op jit(solution)/shard_map/over_leaf/all_to_all | solution.py:187
  110.0 0.0 collective-permute-done.13
  110.1 0.0 collective-permute-done.14
  110.1 0.0 copy-start.3
  110.1 0.0 copy-start.8
  110.1 6.4 %all-to-all-done.2.y_ref = bf16[8,64,256]{2,1,0:T(8,128)(2,1)S(1)} async-done(((bf16[8,64,256]{2,1,0:T(8,128)(2,1)}), bf16[8,64,256]{2,1,0:T(8,128)(2,1)S(1)}, u32[]{:S(2)}, u32[]{:S(2)}) %all-to-all-start.2) | async-done | bytes 262176 | tf_op jit(solution)/shard_map/over_leaf/all_to_all | solution.py:187
  116.5 0.7 copy-done.2
  117.2 6.5 %recur.1 = bf16[64,256]{1,0:T(8,128)(2,1)} custom-call(s32[9]{0:T(128)} %pad_add_fusion.at_ref, bf16[8,64,256]{2,1,0:T(8,128)(2,1)} %copy-done.2, f32[8,64,384]{2,1,0:T(8,128)} %copy-done.3), custom_call_target="tpu_custom_call" | custom-call | tf_op jit(solution)/shard_map/recur/pallas_call | solution.py:129
  123.8 1.8 broadcast_in_dim.36
  125.6 7.4 %all-to-all-start.3 = ((bf16[32,64,256]{2,1,0:T(8,128)(2,1)}), bf16[32,64,256]{2,1,0:T(8,128)(2,1)S(1)}, u32[]{:S(2)}, u32[]{:S(2)}) async-start(bf16[32,64,256]{2,1,0:T(8,128)(2,1)} %broadcast_in_dim.36), calls=%async_computation.3 | async-start | bytes 2097152 | tf_op jit(solution)/shard_map/over_node/all_to_all | solution.py:187
  133.0 1.5 collective-permute-start.3
  134.5 2.4 %collective-permute-start.4 = (bf16[512,512]{1,0:T(8,128)(2,1)}, bf16[512,512]{1,0:T(8,128)(2,1)S(1)}, u32[]{:S(2)}, u32[]{:S(2)}) collective-permute-start(bf16[512,512]{1,0:T(8,128)(2,1)} %get-tuple-element.16), channel_id=1, source_target_pairs={{0,2},{1,3},{2,0},{3,1},{4,6},{5,7},{6,4},{7,5},{8,10},{9,11},{10,... | collective-permute-start | bytes 1572872 | tf_op jit(solution)/shard_map/move_x/ppermute | solution.py:178
  136.9 1.2 collective-permute-start.5
  138.1 8.0 %scatter_custom_fusion = s32[2048]{0:T(1024)S(1)} fusion(s32[2048]{0:T(1024)S(1)} %get-tuple-element.26, s32[2048]{0:T(1024)S(1)} %get-tuple-element.27, s32[]{:T(128)} %constant.123.clone.1), kind=kCustom, calls=%fused_computation.45 | custom fusion | bytes 8196 | tf_op jit(solution)/shard_map/columns/scatter | solution.py:236
  146.1 9.7 %collective-permute-done.3.v1 = bf16[512,512]{1,0:T(8,128)(2,1)S(1)} collective-permute-done((bf16[512,512]{1,0:T(8,128)(2,1)}, bf16[512,512]{1,0:T(8,128)(2,1)S(1)}, u32[]{:S(2)}, u32[]{:S(2)}) %collective-permute-start.3) | collective-permute-done | bytes 524320 | tf_op jit(solution)/shard_map/move_x/ppermute | solution.py:178
  155.8 14.0 %collective-permute-done.4.v2 = bf16[512,512]{1,0:T(8,128)(2,1)S(1)} collective-permute-done((bf16[512,512]{1,0:T(8,128)(2,1)}, bf16[512,512]{1,0:T(8,128)(2,1)S(1)}, u32[]{:S(2)}, u32[]{:S(2)}) %collective-permute-start.4) | collective-permute-done | bytes 524320 | tf_op jit(solution)/shard_map/move_x/ppermute | solution.py:178
  169.8 1.1 collective-permute-done.5.v3
  170.9 0.0 all-to-all-done.3
  170.9 0.8 copy-done.6
  171.7 0.4 copy-done.1
  172.1 7.1 %finish.1 = (bf16[2048,512]{1,0:T(8,128)(2,1)}, bf16[512,128]{1,0:T(8,128)(2,1)}) custom-call(s32[1]{0:T(128)} %bitcast.x_ref, bf16[512,512]{1,0:T(8,128)(2,1)} %get-tuple-element.14.v0, bf16[512,512]{1,0:T(8,128)(2,1)} %copy-done.4, bf16[512,512]{1,0:T(8,128)(2,1)} %copy-done.5, bf16[512,512]{1,0:T(8,128)(2,1)} %copy-done.6, ...), custom_call_target="tpu_custom_call" | custom-call | tf_op jit(solution)/shard_map/finish/pallas_call | solution.py:164
  179.2 7.0 %all-to-all-start.4 = ((bf16[32,16,128]{2,1,0:T(8,128)(2,1)}), bf16[32,16,128]{2,1,0:T(8,128)(2,1)S(1)}, u32[]{:S(2)}, u32[]{:S(2)}) async-start(bf16[32,16,128]{2,1,0:T(8,128)(2,1)} %bitcast.26), calls=%async_computation.4 | async-start | bytes 262144 | tf_op jit(solution)/shard_map/cells/all_to_all | solution.py:229
  186.2 9.5 %gather_fusion = bf16[2048,512]{1,0:T(8,128)(2,1)S(1)} fusion(bf16[2048,512]{1,0:T(8,128)(2,1)} %get-tuple-element.22, s32[2048]{0:T(1024)S(1)} %fusion.18), kind=kCustom, calls=%fused_computation | custom fusion | bytes 4202496 | tf_op jit(solution)/shard_map/columns/jit(_take)/gather | solution.py:237
  195.7 0.0 all-to-all-done.4
  195.7 0.6 broadcast_in_dim.39
  196.3 5.5 %all-to-all-start.5 = ((f32[8,16,128]{2,1,0:T(8,128)}), f32[8,16,128]{2,1,0:T(8,128)S(1)}, u32[]{:S(2)}, u32[]{:S(2)}) async-start(f32[8,16,128]{2,1,0:T(8,128)} %broadcast_in_dim.39), calls=%async_computation.5 | async-start | bytes 131072 | tf_op jit(solution)/shard_map/cells/all_to_all | solution.py:187
  201.8 1.5 broadcast_select_fusion
  203.4 3.3 %all-to-all-done.5 = f32[8,16,128]{2,1,0:T(8,128)S(1)} async-done(((f32[8,16,128]{2,1,0:T(8,128)}), f32[8,16,128]{2,1,0:T(8,128)S(1)}, u32[]{:S(2)}, u32[]{:S(2)}) %all-to-all-start.5) | async-done | bytes 65568 | tf_op jit(solution)/shard_map/cells/all_to_all | solution.py:187
  206.7 0.6 reduce_sum.32
  (25 shorter events, 0.3 us)
Async XLA Ops:
  3.8 77.0 %all-to-all-start = ((bf16[8,64,2048]{2,1,0:T(8,128)(2,1)}), bf16[8,64,2048]{2,1,0:T(8,128)(2,1)S(1)}, u32[]{:S(2)}, u32[]{:S(2)}) async-start(bf16[8,64,2048]{2,1,0:T(8,128)(2,1)} %bitcast.20), calls=%async_computation | async-start | bytes 4194304 | tf_op jit(solution)/shard_map/move_z/all_to_all | solution.py:199
  15.3 4.0 %collective-permute-start.6 = (f32[64,384]{1,0:T(8,128)}, f32[64,384]{1,0:T(8,128)S(1)}, u32[]{:S(2)}, u32[]{:S(2)}) collective-permute-start(f32[64,384]{1,0:T(8,128)} %get-tuple-element.19), channel_id=1, source_target_pairs={{0,1},{1,0},{2,3},{3,2},{4,5},{5,4},{6,7},{7,6},{8,9},{9,8},{10,11... | collective-permute-start | bytes 294920 | tf_op jit(solution)/shard_map/maps/ppermute | solution.py:182
  20.2 5.4 %collective-permute-start.7 = (f32[64,384]{1,0:T(8,128)S(1)}, f32[64,384]{1,0:T(8,128)S(1)}, u32[]{:S(2)}, u32[]{:S(2)}) collective-permute-start(f32[64,384]{1,0:T(8,128)S(1)} %add.93), channel_id=1, source_target_pairs={{0,2},{1,3},{2,0},{3,1},{4,6},{5,7},{6,4},{7,5},{8,10},{9,11},{10,... | collective-permute-start | bytes 294920 | tf_op jit(solution)/shard_map/maps/ppermute | solution.py:182
  25.6 35.8 %collective-permute-start.8 = (f32[64,384]{1,0:T(8,128)S(1)}, f32[64,384]{1,0:T(8,128)S(1)}, u32[]{:S(2)}, u32[]{:S(2)}) collective-permute-start(f32[64,384]{1,0:T(8,128)S(1)} %add.94), channel_id=1, source_target_pairs={{0,4},{4,0},{8,12},{12,8},{16,20},{20,16},{24,28},{28,24},{1,5},{5... | collective-permute-start | bytes 294920 | tf_op jit(solution)/shard_map/maps/ppermute | solution.py:182
  61.4 8.0 %collective-permute-start.9 = (f32[64,384]{1,0:T(8,128)S(1)}, f32[64,384]{1,0:T(8,128)S(1)}, u32[]{:S(2)}, u32[]{:S(2)}) collective-permute-start(f32[64,384]{1,0:T(8,128)S(1)} %add.95), channel_id=1, source_target_pairs={{0,8},{4,12},{8,0},{12,4},{16,24},{20,28},{24,16},{28,20},{1,9},{5... | collective-permute-start | bytes 294920 | tf_op jit(solution)/shard_map/maps/ppermute | solution.py:182
  62.7 18.1 %collective-permute-start = (bf16[256,512]{1,0:T(8,128)(2,1)}, bf16[256,512]{1,0:T(8,128)(2,1)S(1)}, u32[]{:S(2)}, u32[]{:S(2)}) collective-permute-start(bf16[256,512]{1,0:T(8,128)(2,1)} %get-tuple-element.13.w0), channel_id=1, source_target_pairs={{0,1},{1,2},{2,3},{3,0},{4,5},{5,6},{6,7},{7,4},{8,9},{9,10},{10,1... | collective-permute-start | bytes 786440 | tf_op jit(solution)/shard_map/maps/ppermute | solution.py:178
  63.9 16.9 %collective-permute-start.1 = (bf16[256,512]{1,0:T(8,128)(2,1)}, bf16[256,512]{1,0:T(8,128)(2,1)}, u32[]{:S(2)}, u32[]{:S(2)}) collective-permute-start(bf16[256,512]{1,0:T(8,128)(2,1)} %get-tuple-element.13.w0), channel_id=1, source_target_pairs={{0,2},{1,3},{2,0},{3,1},{4,6},{5,7},{6,4},{7,5},{8,10},{9,11},{10,... | collective-permute-start | bytes 786440 | tf_op jit(solution)/shard_map/maps/ppermute | solution.py:178
  66.4 14.4 %collective-permute-start.2 = (bf16[256,512]{1,0:T(8,128)(2,1)}, bf16[256,512]{1,0:T(8,128)(2,1)}, u32[]{:S(2)}, u32[]{:S(2)}) collective-permute-start(bf16[256,512]{1,0:T(8,128)(2,1)} %get-tuple-element.13.w0), channel_id=1, source_target_pairs={{0,3},{1,0},{2,1},{3,2},{4,7},{5,4},{6,5},{7,6},{8,11},{9,8},{10,9... | collective-permute-start | bytes 786440 | tf_op jit(solution)/shard_map/maps/ppermute | solution.py:178
  69.4 7.5 %collective-permute-start.10 = (f32[64,384]{1,0:T(8,128)S(1)}, f32[64,384]{1,0:T(8,128)S(1)}, u32[]{:S(2)}, u32[]{:S(2)}) collective-permute-start(f32[64,384]{1,0:T(8,128)S(1)} %add.96), channel_id=1, source_target_pairs={{0,16},{4,20},{8,24},{12,28},{16,0},{20,4},{24,8},{28,12},{1,17},{... | collective-permute-start | bytes 294920 | tf_op jit(solution)/shard_map/maps/ppermute | solution.py:182
  76.9 15.1 %collective-permute-start.11 = (f32[64,384]{1,0:T(8,128)S(1)}, f32[64,384]{1,0:T(8,128)S(1)}, u32[]{:S(2)}, u32[]{:S(2)}) collective-permute-start(f32[64,384]{1,0:T(8,128)S(1)} %get-tuple-element.25), channel_id=1, source_target_pairs={{0,32},{32,0},{64,96},{96,64},{128,160},{160,128},{192,224},{224,1... | collective-permute-start | bytes 294920 | tf_op jit(solution)/shard_map/maps/ppermute | solution.py:182
  80.8 0.7 copy-start.7
  80.8 1.4 copy-start
  86.1 18.2 %all-to-all-start.1 = ((bf16[8,64,256]{2,1,0:T(8,128)(2,1)}), bf16[8,64,256]{2,1,0:T(8,128)(2,1)S(1)}, u32[]{:S(2)}, u32[]{:S(2)}) async-start(bf16[8,64,256]{2,1,0:T(8,128)(2,1)} %bitcast.25), calls=%async_computation.1 | async-start | bytes 524288 | tf_op jit(solution)/shard_map/sum_z/all_to_all | solution.py:213
  92.0 7.6 %collective-permute-start.12 = (f32[2,64,384]{2,1,0:T(8,128)S(1)}, f32[2,64,384]{2,1,0:T(8,128)S(1)}, u32[]{:S(2)}, u32[]{:S(2)}) collective-permute-start(f32[2,64,384]{2,1,0:T(8,128)S(1)} %pad_maximum_fusion), channel_id=1, source_target_pairs={{0,64},{32,96},{64,128},{96,160},{128,192},{160,224},{192,0},{224,... | collective-permute-start | bytes 589832 | tf_op jit(solution)/shard_map/maps/ppermute | solution.py:178
  93.4 16.7 %collective-permute-start.13 = (f32[2,64,384]{2,1,0:T(8,128)S(1)}, f32[2,64,384]{2,1,0:T(8,128)S(1)}, u32[]{:S(2)}, u32[]{:S(2)}) collective-permute-start(f32[2,64,384]{2,1,0:T(8,128)S(1)} %pad_maximum_fusion), channel_id=1, source_target_pairs={{0,128},{32,160},{64,192},{96,224},{128,0},{160,32},{192,64},{224,... | collective-permute-start | bytes 589832 | tf_op jit(solution)/shard_map/maps/ppermute | solution.py:178
  96.0 14.1 %collective-permute-start.14 = (f32[2,64,384]{2,1,0:T(8,128)S(1)}, f32[2,64,384]{2,1,0:T(8,128)S(1)}, u32[]{:S(2)}, u32[]{:S(2)}) collective-permute-start(f32[2,64,384]{2,1,0:T(8,128)S(1)} %pad_maximum_fusion), channel_id=1, source_target_pairs={{0,192},{32,224},{64,0},{96,32},{128,64},{160,96},{192,128},{224,1... | collective-permute-start | bytes 589832 | tf_op jit(solution)/shard_map/maps/ppermute | solution.py:178
  105.1 11.4 %all-to-all-start.2 = ((bf16[8,64,256]{2,1,0:T(8,128)(2,1)}), bf16[8,64,256]{2,1,0:T(8,128)(2,1)S(1)}, u32[]{:S(2)}, u32[]{:S(2)}) async-start(bf16[8,64,256]{2,1,0:T(8,128)(2,1)} %broadcast_in_dim.35), calls=%async_computation.2 | async-start | bytes 524288 | tf_op jit(solution)/shard_map/over_leaf/all_to_all | solution.py:187
  110.1 6.4 %copy-start.3 = (f32[8,64,384]{2,1,0:T(8,128)}, f32[8,64,384]{2,1,0:T(8,128)S(1)}, u32[]{:S(2)}) copy-start(f32[8,64,384]{2,1,0:T(8,128)S(1)} %constant_dynamic-update-slice_fusion.g_ref) | copy-start | bytes 2359300
  110.1 27.9 %copy-start.8 = (s32[2048]{0:T(1024)S(1)}, s32[2048]{0:T(1024)}, u32[]{:S(2)}) copy-start(s32[2048]{0:T(1024)} %param.14) | copy-start | bytes 24580
  116.5 0.7 copy-start.2
  125.6 45.3 %all-to-all-start.3 = ((bf16[32,64,256]{2,1,0:T(8,128)(2,1)}), bf16[32,64,256]{2,1,0:T(8,128)(2,1)S(1)}, u32[]{:S(2)}, u32[]{:S(2)}) async-start(bf16[32,64,256]{2,1,0:T(8,128)(2,1)} %broadcast_in_dim.36), calls=%async_computation.3 | async-start | bytes 2097152 | tf_op jit(solution)/shard_map/over_node/all_to_all | solution.py:187
  133.0 22.8 %collective-permute-start.3 = (bf16[512,512]{1,0:T(8,128)(2,1)}, bf16[512,512]{1,0:T(8,128)(2,1)S(1)}, u32[]{:S(2)}, u32[]{:S(2)}) collective-permute-start(bf16[512,512]{1,0:T(8,128)(2,1)} %get-tuple-element.15), channel_id=1, source_target_pairs={{0,1},{1,2},{2,3},{3,0},{4,5},{5,6},{6,7},{7,4},{8,9},{9,10},{10,1... | collective-permute-start | bytes 1572872 | tf_op jit(solution)/shard_map/move_x/ppermute | solution.py:178
  134.5 35.4 %collective-permute-start.4 = (bf16[512,512]{1,0:T(8,128)(2,1)}, bf16[512,512]{1,0:T(8,128)(2,1)S(1)}, u32[]{:S(2)}, u32[]{:S(2)}) collective-permute-start(bf16[512,512]{1,0:T(8,128)(2,1)} %get-tuple-element.16), channel_id=1, source_target_pairs={{0,2},{1,3},{2,0},{3,1},{4,6},{5,7},{6,4},{7,5},{8,10},{9,11},{10,... | collective-permute-start | bytes 1572872 | tf_op jit(solution)/shard_map/move_x/ppermute | solution.py:178
  136.9 34.0 %collective-permute-start.5 = (bf16[512,512]{1,0:T(8,128)(2,1)}, bf16[512,512]{1,0:T(8,128)(2,1)S(1)}, u32[]{:S(2)}, u32[]{:S(2)}) collective-permute-start(bf16[512,512]{1,0:T(8,128)(2,1)} %get-tuple-element.17), channel_id=1, source_target_pairs={{0,3},{1,0},{2,1},{3,2},{4,7},{5,4},{6,5},{7,6},{8,11},{9,8},{10,9... | collective-permute-start | bytes 1572872 | tf_op jit(solution)/shard_map/move_x/ppermute | solution.py:178
  155.8 15.1 %copy-start.4 = (bf16[512,512]{1,0:T(8,128)(2,1)}, bf16[512,512]{1,0:T(8,128)(2,1)S(1)}, u32[]{:S(2)}) copy-start(bf16[512,512]{1,0:T(8,128)(2,1)S(1)} %collective-permute-done.3.v1) | copy-start | bytes 1572868
  169.8 1.1 copy-start.5
  170.9 0.8 copy-start.6
  170.9 1.2 copy-start.1
  179.2 16.5 %all-to-all-start.4 = ((bf16[32,16,128]{2,1,0:T(8,128)(2,1)}), bf16[32,16,128]{2,1,0:T(8,128)(2,1)S(1)}, u32[]{:S(2)}, u32[]{:S(2)}) async-start(bf16[32,16,128]{2,1,0:T(8,128)(2,1)} %bitcast.26), calls=%async_computation.4 | async-start | bytes 262144 | tf_op jit(solution)/shard_map/cells/all_to_all | solution.py:229
  196.3 10.4 %all-to-all-start.5 = ((f32[8,16,128]{2,1,0:T(8,128)}), f32[8,16,128]{2,1,0:T(8,128)S(1)}, u32[]{:S(2)}, u32[]{:S(2)}) async-start(f32[8,16,128]{2,1,0:T(8,128)} %broadcast_in_dim.39), calls=%async_computation.5 | async-start | bytes 131072 | tf_op jit(solution)/shard_map/cells/all_to_all | solution.py:187
where the time goes:
time: 208 us; the launch traced here: 207 us
  waiting for transfers between devices  89.1 us (43%)
  starting transfers between devices  66.4 us (32%)
  local copies, waits for them, and re-layouts  27.2 us (13%)
  Pallas kernels  20.1 us (10%)
  other arithmetic  3.81 us (2%)
    ppermute x6, waiting for transfers between devices, swapped(): lax.ppermute(a, axis, [(i, i ^ bit) for i in range(lax.axis_size(axis))])  47.3 us
    ppermute x9, waiting for transfers between devices, shifted(): return lax.ppermute(a, axis, [(i, (i + by) % count) for i in range(count)])  27.3 us
    all_to_all x3, starting transfers between devices, broadcast(): lax.all_to_all(jnp.broadcast_to(a[None], (count, *a.shape)), axes, 0, 0,...  17.8 us
    ppermute x9, starting transfers between devices, shifted(): return lax.ppermute(a, axis, [(i, (i + by) % count) for i in range(count)])  14.9 us
    ppermute x6, starting transfers between devices, swapped(): lax.ppermute(a, axis, [(i, i ^ bit) for i in range(lax.axis_size(axis))])  11.7 us
    all_to_all x3, waiting for transfers between devices, broadcast(): lax.all_to_all(jnp.broadcast_to(a[None], (count, *a.shape)), axes, 0, 0,...  9.74 us
    gather x1, local copies, waits for them, and re-layouts, per_device(): solution = jnp.take(sol, source_row, axis=0)  9.45 us
    all_to_all x1, starting transfers between devices, per_device(): lax.all_to_all(by_z, 'z', 0, 0, tiled=True).reshape(NZ * shots, NX * BLOCK)  9 us
  transfers between devices with their start and end apart: 21, of which 12 were waited for; matrix products, arithmetic and copies ran while one was open for 10% of the time, Pallas kernels for 3%

commit v1 on v0

v1 whole, which is shorter than its diff:
```python
import jax
import jax.numpy as jnp
from jax import lax
from jax.experimental import pallas as pl
from jax.experimental.pallas import tpu as pltpu
from jax.sharding import Mesh, PartitionSpec as P


BLOCK = 512
RANK = 64
NZ = 8
NX = 4
NLEAF = 8
LANES = 128
BF = jnp.bfloat16
F32 = jnp.float32
NT = (((1,), (1,)), ((), ()))
VMEM_SPEC = pl.BlockSpec(memory_space=pltpu.VMEM)
SMEM_SPEC = pl.BlockSpec(memory_space=pltpu.SMEM)


def dot(a, b):
    return jnp.dot(a.astype(BF), b.astype(BF), preferred_element_type=F32)


def dot_nt(a, b):
    return lax.dot_general(a.astype(BF), b.astype(BF), NT, preferred_element_type=F32)


def prepare_kernel(d_ref, left_ref, right_ref, cin_ref, cout_ref, w_ref, g_ref, back_ref):
    d = d_ref[...]
    right = right_ref[...]
    cin = cin_ref[...]
    both = jnp.concatenate([right, cout_ref[...]], axis=0)
    cin_d = dot(cin, d)
    w_ref[0:64, :] = left_ref[...]
    w_ref[64:192, :] = dot_nt(both, d).astype(BF)
    w_ref[192:256, :] = dot_nt(cin_d, d).astype(BF)
    g_ref[:, 0:256] = dot_nt(cin, w_ref[...])
    g_ref[:, 256:384] = dot_nt(right, both)
    back_ref[...] = cin_d.astype(BF)


def prepare(d, left, right, cin, cout):
    return pl.pallas_call(
        prepare_kernel,
        name="prepare",
        out_shape=(
            jax.ShapeDtypeStruct((4 * RANK, BLOCK), BF),
            jax.ShapeDtypeStruct((RANK, 6 * RANK), F32),
            jax.ShapeDtypeStruct((RANK, BLOCK), BF),
        ),
        in_specs=[VMEM_SPEC] * 5,
        out_specs=(VMEM_SPEC,) * 3,
    )(d, left, right, cin, cout)


def project_kernel(x_ref, v_ref, w0, w1, w2, w3, g_ref, y_ref, p0, p1, p2, p3, g_out):
    x = x_ref[0]
    total = None
    for k, w in enumerate((w0, w1, w2, w3)):
        at = pl.multiple_of(lax.rem(x + (NX - k), NX) * BLOCK, BLOCK)
        part = lax.dot_general(v_ref[:, pl.ds(at, BLOCK)], w[...], NT, preferred_element_type=F32)
        total = part if total is None else total + part
    y_ref[...] = total.astype(BF)
    for k, piece in enumerate((p0, p1, p2, p3)):
        at = pl.multiple_of(lax.rem(x + k, NX) * BLOCK, BLOCK)
        piece[...] = v_ref[:, pl.ds(at, BLOCK)]
    g_out[...] = g_ref[...]


def project(x, v, ws, g):
    rows = v.shape[0]
    return pl.pallas_call(
        project_kernel,
        name="project",
        out_shape=(jax.ShapeDtypeStruct((rows, 4 * RANK), BF),)
        + (jax.ShapeDtypeStruct((rows, BLOCK), BF),) * NX
        + (jax.ShapeDtypeStruct(g.shape, g.dtype),),
        in_specs=[SMEM_SPEC] + [VMEM_SPEC] * 6,
        out_specs=(VMEM_SPEC,) * 6,
    )(x, v, *ws, g)


def total_kernel(part_ref, own_ref, early_ref):
    own = part_ref[0].astype(F32)
    for i in range(1, NZ):
        own += part_ref[i].astype(F32)
    own = own.astype(BF)
    own_ref[...] = own
    for i in range(NZ * NX):
        early_ref[i] = own[:, 0:128]


def total(parts):
    shots = parts.shape[1]
    return pl.pallas_call(
        total_kernel,
        name="total",
        out_shape=(
            jax.ShapeDtypeStruct((shots, 4 * RANK), BF),
            jax.ShapeDtypeStruct((NZ * NX, shots, 2 * RANK), BF),
        ),
        in_specs=[VMEM_SPEC],
        out_specs=(VMEM_SPEC,) * 2,
    )(parts)


def cols(a, i):
    return a[:, i * RANK : (i + 1) * RANK]


def lowrank_kernel(g_ref, d_ref, left_ref, right_ref, cin_d_ref, cout_ref, wf_ref, ws_ref):
    p, s2, _, _, m2, m1 = (cols(g_ref[...], i) for i in range(6))
    left = left_ref[...]
    right = right_ref[...]
    zero = jnp.zeros((RANK, BLOCK), BF)
    wf_ref[0:64, :] = right
    wf_ref[64:128, :] = zero
    wf_ref[128:192, :] = (-(cin_d_ref[...].astype(F32) + dot(p, right))).astype(BF)
    wf_ref[192:256, :] = zero
    ws_ref[0:64, :] = dot(m2, left).astype(BF)
    ws_ref[64:128, :] = left
    ws_ref[128:192, :] = (-dot(s2 + dot(p, m2), left)).astype(BF)
    ws_ref[192:256, :] = (-(dot_nt(cout_ref[...], d_ref[...]) + dot(m1.T, left))).astype(BF)


def lowrank(g, d, left, right, cin_d, cout):
    return pl.pallas_call(
        lowrank_kernel,
        name="lowrank",
        out_shape=(jax.ShapeDtypeStruct((4 * RANK, BLOCK), BF),) * 2,
        in_specs=[VMEM_SPEC] * 6,
        out_specs=(VMEM_SPEC,) * 2,
    )(g, d, left, right, cin_d, cout)


def recur_kernel(at_ref, f0, f1, f2, f3, out_ref, all_ref):
    for k, f in enumerate((f0, f1, f2, f3)):
        all_ref[pl.ds(2 * k, 2)] = f[...]
    mine = at_ref[0]
    zero = jnp.zeros((f0.shape[1], RANK), F32)
    inc = inc_mine = zero
    steps, lifts = [], []
    for j in range(NLEAF):
        both = all_ref[at_ref[1 + j]]
        maps = both[:, 256:640].astype(F32)
        p, s2, s1, s4, m2, m1 = (cols(maps, i) for i in range(6))
        y = both[:, 0:256].astype(F32)
        proj, y_q, y_carry, y_lift = (cols(y, i) for i in range(4))
        step = -(s1 + dot(p, m1))
        q_map = s2 + dot(p, m2)
        lift_map = s4 + dot_nt(p, s2)
        q = y_q + dot(proj, m2) - dot(inc, q_map)
        lift = y_lift + dot_nt(proj, s2) - dot(inc, lift_map) + dot_nt(q, p)
        inc_mine = jnp.where(mine == j, inc, inc_mine)
        inc = y_carry + dot(proj, m1) + dot(inc, step)
        steps.append(step)
        lifts.append(lift)
    ret = ret_mine = zero
    for j in range(NLEAF - 1, -1, -1):
        ret_mine = jnp.where(mine == j, ret, ret_mine)
        if j:
            ret = lifts[j] + dot_nt(ret, steps[j])
    late = jnp.concatenate([inc_mine, ret_mine], axis=1).astype(BF)
    for i in range(NZ * NX):
        out_ref[i] = late


def recur(at, far):
    shots = far[0].shape[1]
    return pl.pallas_call(
        recur_kernel,
        name="recur",
        out_shape=jax.ShapeDtypeStruct((NZ * NX, shots, 2 * RANK), BF),
        in_specs=[SMEM_SPEC] + [VMEM_SPEC] * 4,
        out_specs=VMEM_SPEC,
        scratch_shapes=[pltpu.VMEM((NLEAF, *far[0].shape[1:]), BF)],
    )(at, *far)


def finish_kernel(
    x_ref, v0, v1, v2, v3, early_ref, late_ref, d_ref, wf_ref, ws_ref, map_ref, sol_ref, cell_ref
):
    x = x_ref[0]
    rows = v0.shape[0]
    corr = jnp.zeros((1, BLOCK), F32)
    for k, v in enumerate((v0, v1, v2, v3)):
        node = lax.rem(x + (NX - k), NX)
        coef = jnp.concatenate(
            [r[:, node].reshape(rows, 2 * RANK) for r in (early_ref, late_ref)], axis=1
        )
        fwd = dot(v[...], d_ref[...]) + dot(coef, wf_ref[...])
        fwd = fwd.astype(BF)
        sol = dot_nt(fwd, d_ref[...]) + dot(coef, ws_ref[...])
        sol = sol.astype(BF)
        sol_ref[pl.ds(k * rows, rows), :] = sol
        corr += jnp.sum(sol.astype(F32) * fwd.astype(F32), axis=0, keepdims=True)
    corr = corr * (1.0 / jnp.sqrt(F32(NX * rows)))
    cell = map_ref[...]
    count = cell_ref.shape[0]
    high = lax.broadcasted_iota(jnp.int32, (count, BLOCK), 0) == cell // LANES
    low = lax.broadcasted_iota(jnp.int32, (LANES, BLOCK), 0) == cell % LANES
    hot = jnp.where(low, 1.0, 0.0).astype(BF)
    first = corr.astype(BF).astype(F32)
    cells = dot_nt(jnp.where(high, first, 0.0), hot) + dot_nt(jnp.where(high, corr - first, 0.0), hot)
    cell_ref[...] = cells.astype(BF)


def finish(x, vs, early, late, d, wf, ws, cells, cell_rows):
    rows = vs[0].shape[0]
    return pl.pallas_call(
        finish_kernel,
        name="finish",
        out_shape=(
            jax.ShapeDtypeStruct((NX * rows, BLOCK), BF),
            jax.ShapeDtypeStruct((cell_rows, LANES), BF),
        ),
        in_specs=[SMEM_SPEC] + [VMEM_SPEC] * 10,
        out_specs=(VMEM_SPEC,) * 2,
    )(x, *vs, early, late, d, wf, ws, cells)


def shifted(a, axis, by):
    count = lax.axis_size(axis)
    return lax.ppermute(a, axis, [(i, (i + by) % count) for i in range(count)])


def swapped(a, axis, bit):
    return lax.ppermute(a, axis, [(i, i ^ bit) for i in range(lax.axis_size(axis))])


def broadcast(a, axes):
    count = lax.axis_size(axes)
    return lax.all_to_all(jnp.broadcast_to(a[None], (count, *a.shape)), axes, 0, 0, tiled=True)


def per_device(
    sources, block_inverse, basis_left, basis_right, couple_in, couple_out, column_of_shot, cell_map
):
    node = ("z", "x")
    shots = sources.shape[0]
    _, x, leaf = (lax.axis_index(a) for a in ("z", "x", "leaf"))
    y, core = leaf // 2, leaf % 2
    by_z = jnp.swapaxes(sources.reshape(shots, NZ, NX * BLOCK), 0, 1)
    v = lax.all_to_all(by_z, "z", 0, 0, tiled=True).reshape(NZ * shots, NX * BLOCK)
    w, g, cin_d = prepare(block_inverse, basis_left, basis_right, couple_in, couple_out)
    ws = [w] + [shifted(w, "x", k) for k in range(1, NX)]
    for bit in (1, 2):
        g = g + swapped(g, "x", bit)
    here = x.reshape(1).astype(jnp.int32)
    part, *pieces, g = project(here, v, ws, g)
    parts = lax.all_to_all(part.reshape(NZ, shots, 4 * RANK), "z", 0, 0, tiled=True)
    vs = [pieces[0]] + [shifted(pieces[k], "x", k) for k in range(1, NX)]
    for bit in (1, 2, 4):
        g = g + swapped(g, "z", bit)
    wf, ws = lowrank(g, block_inverse, basis_left, basis_right, cin_d, couple_out)
    own, early = total(parts)
    early = lax.all_to_all(early, node, 0, 0, tiled=True)
    own = jnp.concatenate([own, g.astype(BF)], axis=1)
    pair = jnp.stack([own, swapped(own, "leaf", 1)])
    far = [pair] + [shifted(pair, "leaf", 2 * k) for k in range(1, NLEAF // 2)]
    group = jnp.arange(NLEAF, dtype=jnp.int32)
    place = ((y - group // 2) % (NLEAF // 2)) * 2 + (group % 2 + core) % 2
    at = jnp.concatenate([leaf.reshape(1), place]).astype(jnp.int32)
    late = recur(at, far)
    late = lax.all_to_all(late, node, 0, 0, tiled=True)
    early, late = (a.reshape(NZ, NX, shots, 2 * RANK) for a in (early, late))
    cell_rows = NZ * NX * 2048 // LANES
    sol, cells = finish(
        here, vs, early, late, block_inverse, wf, ws, cell_map.reshape(1, BLOCK), cell_rows
    )
    parts = cells.reshape(NZ * NX, cell_rows // (NZ * NX), LANES)
    parts = lax.all_to_all(parts, node, 0, 0, tiled=True)
    slab = parts.astype(F32).sum(axis=0)
    gradient = broadcast(slab, "leaf").sum(axis=0).reshape(-1)
    shot = jnp.arange(NZ * NX * shots, dtype=jnp.int32)
    from_node = shot // shots
    row = ((x - from_node % NX) % NX) * (NZ * shots) + (from_node // NX) * shots + shot % shots
    source_row = jnp.zeros_like(row).at[column_of_shot].set(row)
    solution = jnp.take(sol, source_row, axis=0)
    return solution, gradient


def solution(mesh):
    split = Mesh(mesh.devices.reshape(NLEAF, NZ, NX), ("leaf", "z", "x"))
    block = P(None, ("leaf", "z", "x"))
    return jax.shard_map(
        per_device,
        mesh=split,
        in_specs=(
            P(("z", "x"), "leaf"),
            block,
            block,
            block,
            block,
            block,
            P(),
            P(("leaf", "z", "x")),
        ),
        out_specs=(block, P(("z", "x"))),
        check_vma=False,
    )
```

time: 208 us -> 220 us (1.058)
  Pallas kernels: 20.1 us -> 24.5 us
  waiting for transfers between devices: 89.1 us -> 92.2 us
  other arithmetic: 3.81 us -> 6.75 us
  starting transfers between devices: 66.4 us -> 69.1 us
    all_to_all x1, waiting for transfers between devices: 0.01 us -> 25.8 us  [per_device(): lax.all_to_all(by_z, 'z', 0, 0, tiled=True).reshape(NZ * shots, NX * BLOCK)]
    ppermute x6, waiting for transfers between devices: 47.3 us -> 30.8 us  [swapped(): lax.ppermute(a, axis, [(i, i ^ bit) for i in range(lax.axis_size(axis))])]
    all_to_all x0 -> x2, starting transfers between devices: none -> 12.2 us  [the longest x1 7.82 us: per_device(): late = lax.all_to_all(late, node, 0, 0, tiled=True)]
    all_to_all x3 -> x1, starting transfers between devices: 17.8 us -> 5.68 us  [broadcast(): lax.all_to_all(jnp.broadcast_to(a[None], (count, *a.shape)), axes, 0, 0,...]
    all_to_all x3 -> x1, waiting for transfers between devices: 9.74 us -> 3.35 us  [broadcast(): lax.all_to_all(jnp.broadcast_to(a[None], (count, *a.shape)), axes, 0, 0,...]
    all_to_all x1, waiting for transfers between devices: 4.73 us -> 10.4 us  [per_device(): lax.all_to_all(part.reshape(NZ, shots, 4 * RANK), 'z', 0, 0, tiled=True)]
    ppermute x9, waiting for transfers between devices: 27.3 us -> 21.8 us  [shifted(): return lax.ppermute(a, axis, [(i, (i + by) % count) for i in range(count)])]
    ppermute x6, starting transfers between devices: 11.7 us -> 16 us  [swapped(): lax.ppermute(a, axis, [(i, i ^ bit) for i in range(lax.axis_size(axis))])]
  transfers between devices with their start and end apart: 21 -> 21, of which waited for: 12 -> 12; matrix products, arithmetic and copies ran while one was open for 10% -> 11% of each run, Pallas kernels for 3% -> 6%
where the time goes in v1:
time: 220 us; the launch traced here: 219 us
  waiting for transfers between devices  92.2 us (42%)
  starting transfers between devices  69.1 us (31%)
  local copies, waits for them, and re-layouts  25.7 us (12%)
  Pallas kernels  24.5 us (11%)
  other arithmetic  6.75 us (3%)
    ppermute x6, waiting for transfers between devices, swapped(): lax.ppermute(a, axis, [(i, i ^ bit) for i in range(lax.axis_size(axis))])  30.8 us
    all_to_all x1, waiting for transfers between devices, per_device(): lax.all_to_all(by_z, 'z', 0, 0, tiled=True).reshape(NZ * shots, NX * BLOCK)  25.8 us
    ppermute x9, waiting for transfers between devices, shifted(): return lax.ppermute(a, axis, [(i, (i + by) % count) for i in range(count)])  21.8 us
    ppermute x6, starting transfers between devices, swapped(): lax.ppermute(a, axis, [(i, i ^ bit) for i in range(lax.axis_size(axis))])  16 us
    ppermute x9, starting transfers between devices, shifted(): return lax.ppermute(a, axis, [(i, (i + by) % count) for i in range(count)])  14.9 us
    all_to_all x1, waiting for transfers between devices, per_device(): lax.all_to_all(part.reshape(NZ, shots, 4 * RANK), 'z', 0, 0, tiled=True)  10.4 us
    gather x1, local copies, waits for them, and re-layouts, per_device(): solution = jnp.take(sol, source_row, axis=0)  9.45 us
    all_to_all x1, starting transfers between devices, per_device(): lax.all_to_all(by_z, 'z', 0, 0, tiled=True).reshape(NZ * shots, NX * BLOCK)  9 us
  transfers between devices with their start and end apart: 21, of which 12 were waited for; matrix products, arithmetic and copies ran while one was open for 11% of the time, Pallas kernels for 6%

profile of v1, /device:TPU:1, one launch (start us, length us, event | category | flops | bytes accessed | tf_op | source)
XLA Modules:
  0.0 219.1 jit_solution(14007155238751296442)
XLA Ops:
  0.6 3.2 %copy.14 = bf16[8,8,8,2048]{3,2,0,1:T(8,128)(2,1)} copy(bf16[8,8,8,2048]{3,2,1,0:T(8,128)(2,1)} %bitcast.21) | data formatting | bytes 4194304 | tf_op jit(solution)/shard_map/reshape | solution.py:245
  3.8 9.0 %all-to-all-start = ((bf16[8,64,2048]{2,1,0:T(8,128)(2,1)}), bf16[8,64,2048]{2,1,0:T(8,128)(2,1)S(1)}, u32[]{:S(2)}, u32[]{:S(2)}) async-start(bf16[8,64,2048]{2,1,0:T(8,128)(2,1)} %bitcast.20), calls=%async_computation | async-start | bytes 4194304 | tf_op jit(solution)/shard_map/all_to_all | solution.py:246
  12.8 2.5 %prepare.1 = (bf16[256,512]{1,0:T(8,128)(2,1)}, f32[64,384]{1,0:T(8,128)}, bf16[64,512]{1,0:T(8,128)(2,1)}) custom-call(bf16[512,512]{1,0:T(8,128)(2,1)} %d_ref.5, bf16[64,512]{1,0:T(8,128)(2,1)} %left_ref.3, bf16[64,512]{1,0:T(8,128)(2,1)} %right_ref.3, bf16[64,512]{1,0:T(8,128)(2,1)} %cin_ref.1, bf16[64,512]{1,0:T(8,128)(2,1)} %cout_ref.3), custom_call_target="tpu_custom_call" | custom-call | tf_op jit(solution)/shard_map/prepare/pallas_call | solution.py:45
  15.3 1.2 collective-permute-start
  16.5 2.5 %collective-permute-start.1 = (bf16[256,512]{1,0:T(8,128)(2,1)}, bf16[256,512]{1,0:T(8,128)(2,1)S(1)}, u32[]{:S(2)}, u32[]{:S(2)}) collective-permute-start(bf16[256,512]{1,0:T(8,128)(2,1)} %get-tuple-element.17.w0), channel_id=1, source_target_pairs={{0,2},{1,3},{2,0},{3,1},{4,6},{5,7},{6,4},{7,5},{8,10},{9,11},{10,... | collective-permute-start | bytes 786440 | tf_op jit(solution)/shard_map/ppermute | solution.py:226
  19.0 1.2 collective-permute-start.2
  20.1 0.3 collective-permute-start.3
  20.4 11.3 %collective-permute-done.3 = f32[64,384]{1,0:T(8,128)S(1)} collective-permute-done((f32[64,384]{1,0:T(8,128)}, f32[64,384]{1,0:T(8,128)S(1)}, u32[]{:S(2)}, u32[]{:S(2)}) %collective-permute-start.3) | collective-permute-done | bytes 98336 | tf_op jit(solution)/shard_map/ppermute | solution.py:230
  31.7 0.9 add.86
  32.6 2.9 %collective-permute-start.4 = (f32[64,384]{1,0:T(8,128)S(1)}, f32[64,384]{1,0:T(8,128)S(1)}, u32[]{:S(2)}, u32[]{:S(2)}) collective-permute-start(f32[64,384]{1,0:T(8,128)S(1)} %add.86), channel_id=1, source_target_pairs={{0,2},{1,3},{2,0},{3,1},{4,6},{5,7},{6,4},{7,5},{8,10},{9,11},{10,... | collective-permute-start | bytes 294920 | tf_op jit(solution)/shard_map/ppermute | solution.py:230
  35.5 2.5 %collective-permute-done.4 = f32[64,384]{1,0:T(8,128)S(1)} collective-permute-done((f32[64,384]{1,0:T(8,128)S(1)}, f32[64,384]{1,0:T(8,128)S(1)}, u32[]{:S(2)}, u32[]{:S(2)}) %collective-permute-start.4) | collective-permute-done | bytes 98336 | tf_op jit(solution)/shard_map/ppermute | solution.py:230
  37.9 0.6 add.87.g_ref
  38.6 0.0 collective-permute-done.w1
  38.6 0.0 collective-permute-done.1.w2
  38.6 25.8 %all-to-all-done = bf16[8,64,2048]{2,1,0:T(8,128)(2,1)S(1)} async-done(((bf16[8,64,2048]{2,1,0:T(8,128)(2,1)}), bf16[8,64,2048]{2,1,0:T(8,128)(2,1)S(1)}, u32[]{:S(2)}, u32[]{:S(2)}) %all-to-all-start) | async-done | bytes 2097184 | tf_op jit(solution)/shard_map/all_to_all | solution.py:246
  64.5 1.3 copy-done
  65.8 4.1 %project.1 = (bf16[512,256]{1,0:T(8,128)(2,1)}, bf16[512,512]{1,0:T(8,128)(2,1)}, bf16[512,512]{1,0:T(8,128)(2,1)}, bf16[512,512]{1,0:T(8,128)(2,1)}, bf16[512,512]{1,0:T(8,128)(2,1)}, /*index=5*/f32[64,384]{1,0:T(8,128)}) custom-call(s32[1]{0:T(128)} %bitcast.x_ref, bf16[512,2048]{1,0:T(8,128)(2,1)} %bitcast.19, bf16[256,512]{1,0:T(8,128)(2,1)} %get-tuple-element.17.w0, ...), custom_call_target="tpu_custom_call" | custom-call | tf_op jit(solution)/shard_map/project/pallas_call | solution.py:74
  69.8 3.4 %all-to-all-start.1 = ((bf16[8,64,256]{2,1,0:T(8,128)(2,1)}), bf16[8,64,256]{2,1,0:T(8,128)(2,1)S(1)}, u32[]{:S(2)}, u32[]{:S(2)}) async-start(bf16[8,64,256]{2,1,0:T(8,128)(2,1)} %bitcast.24), calls=%async_computation.1 | async-start | bytes 524288 | tf_op jit(solution)/shard_map/all_to_all | solution.py:253
  73.2 1.4 collective-permute-start.8
  74.6 10.4 %all-to-all-done.1.part_ref = bf16[8,64,256]{2,1,0:T(8,128)(2,1)S(1)} async-done(((bf16[8,64,256]{2,1,0:T(8,128)(2,1)}), bf16[8,64,256]{2,1,0:T(8,128)(2,1)S(1)}, u32[]{:S(2)}, u32[]{:S(2)}) %all-to-all-start.1) | async-done | bytes 262176 | tf_op jit(solution)/shard_map/all_to_all | solution.py:253
  85.0 0.7 copy-done.3
  85.7 1.8 total.1
  87.6 4.4 %all-to-all-start.2 = ((bf16[32,64,128]{2,1,0:T(8,128)(2,1)}), bf16[32,64,128]{2,1,0:T(8,128)(2,1)S(1)}, u32[]{:S(2)}, u32[]{:S(2)}) async-start(bf16[32,64,128]{2,1,0:T(8,128)(2,1)} %get-tuple-element.24), calls=%async_computation.2 | async-start | bytes 1048576 | tf_op jit(solution)/shard_map/all_to_all | solution.py:259
  92.0 0.0 copy-start.14
  92.0 0.0 collective-permute-done.8
  92.0 1.0 add.95
  93.0 2.2 %collective-permute-start.9 = (f32[64,384]{1,0:T(8,128)S(1)}, f32[64,384]{1,0:T(8,128)S(1)}, u32[]{:S(2)}, u32[]{:S(2)}) collective-permute-start(f32[64,384]{1,0:T(8,128)S(1)} %add.95), channel_id=1, source_target_pairs={{0,8},{4,12},{8,0},{12,4},{16,24},{20,28},{24,16},{28,20},{1,9},{5... | collective-permute-start | bytes 294920 | tf_op jit(solution)/shard_map/ppermute | solution.py:230
  95.2 13.5 %collective-permute-done.9 = f32[64,384]{1,0:T(8,128)S(1)} collective-permute-done((f32[64,384]{1,0:T(8,128)S(1)}, f32[64,384]{1,0:T(8,128)S(1)}, u32[]{:S(2)}, u32[]{:S(2)}) %collective-permute-start.9) | collective-permute-done | bytes 98336 | tf_op jit(solution)/shard_map/ppermute | solution.py:230
  108.7 4.8 %collective-permute-start.10 = (f32[64,384]{1,0:T(8,128)S(1)}, f32[64,384]{1,0:T(8,128)S(1)}, u32[]{:S(2)}, u32[]{:S(2)}) collective-permute-start(f32[64,384]{1,0:T(8,128)S(1)} %add.96), channel_id=1, source_target_pairs={{0,16},{4,20},{8,24},{12,28},{16,0},{20,4},{24,8},{28,12},{1,17},{... | collective-permute-start | bytes 294920 | tf_op jit(solution)/shard_map/ppermute | solution.py:230
  113.5 2.7 %collective-permute-done.10 = f32[64,384]{1,0:T(8,128)S(1)} collective-permute-done((f32[64,384]{1,0:T(8,128)S(1)}, f32[64,384]{1,0:T(8,128)S(1)}, u32[]{:S(2)}, u32[]{:S(2)}) %collective-permute-start.10) | collective-permute-done | bytes 98336 | tf_op jit(solution)/shard_map/ppermute | solution.py:230
  116.2 0.6 fusion.28
  116.9 0.8 fusion.27
  117.6 4.4 %collective-permute-start.11 = (bf16[64,640]{1,0:T(8,128)(2,1)S(1)}, bf16[64,640]{1,0:T(8,128)(2,1)S(1)}, u32[]{:S(2)}, u32[]{:S(2)}) collective-permute-start(bf16[64,640]{1,0:T(8,128)(2,1)S(1)} %get-tuple-element.35), channel_id=1, source_target_pairs={{0,32},{32,0},{64,96},{96,64},{128,160},{160,128},{192,224},{224,1... | collective-permute-start | bytes 245768 | tf_op jit(solution)/shard_map/ppermute | solution.py:230
  122.0 0.9 collective-permute-done.11
  122.9 1.4 collective-permute-start.12
  124.3 2.6 %collective-permute-start.13 = (bf16[2,64,640]{2,1,0:T(8,128)(2,1)S(1)}, bf16[2,64,640]{2,1,0:T(8,128)(2,1)S(1)}, u32[]{:S(2)}, u32[]{:S(2)}) collective-permute-start(bf16[2,64,640]{2,1,0:T(8,128)(2,1)S(1)} %pad_maximum_fusion.f0), channel_id=1, source_target_pairs={{0,128},{32,160},{64,192},{96,224},{128,0},{160,32},{192,64},{224,... | collective-permute-start | bytes 491528 | tf_op jit(solution)/shard_map/ppermute | solution.py:226
  126.9 1.1 collective-permute-start.14
  128.0 0.6 pad_add_fusion.at_ref
  128.6 1.2 collective-permute-done.12.f1
  129.8 4.6 %collective-permute-done.13.f2 = bf16[2,64,640]{2,1,0:T(8,128)(2,1)S(1)} collective-permute-done((bf16[2,64,640]{2,1,0:T(8,128)(2,1)S(1)}, bf16[2,64,640]{2,1,0:T(8,128)(2,1)S(1)}, u32[]{:S(2)}, u32[]{:S(2)}) %collective-permute-start.13) | collective-permute-done | bytes 163872 | tf_op jit(solution)/shard_map/ppermute | solution.py:226
  134.4 0.0 collective-permute-done.14.f3
  134.4 0.6 copy-done.12
  135.0 0.7 copy-done.13
  135.7 6.5 %recur.1 = bf16[32,64,128]{2,1,0:T(8,128)(2,1)} custom-call(s32[9]{0:T(128)} %pad_add_fusion.at_ref, bf16[2,64,640]{2,1,0:T(8,128)(2,1)} %copy-done.4, bf16[2,64,640]{2,1,0:T(8,128)(2,1)} %copy-done.11, bf16[2,64,640]{2,1,0:T(8,128)(2,1)} %copy-done.12, bf16[2,64,640]{2,1,0:T(8,128)(2,1)} %copy-done.13), custom_call_target="tpu_custom_call" | custom-call | tf_op jit(solution)/shard_map/recur/pallas_call | solution.py:172
  142.2 7.8 %all-to-all-start.3 = ((bf16[32,64,128]{2,1,0:T(8,128)(2,1)}), bf16[32,64,128]{2,1,0:T(8,128)(2,1)S(1)}, u32[]{:S(2)}, u32[]{:S(2)}) async-start(bf16[32,64,128]{2,1,0:T(8,128)(2,1)} %recur.1), calls=%async_computation.3 | async-start | bytes 1048576 | tf_op jit(solution)/shard_map/all_to_all | solution.py:267
  150.0 1.5 collective-permute-start.5
  151.5 2.4 %collective-permute-start.6 = (bf16[512,512]{1,0:T(8,128)(2,1)}, bf16[512,512]{1,0:T(8,128)(2,1)S(1)}, u32[]{:S(2)}, u32[]{:S(2)}) collective-permute-start(bf16[512,512]{1,0:T(8,128)(2,1)} %get-tuple-element.21), channel_id=1, source_target_pairs={{0,2},{1,3},{2,0},{3,1},{4,6},{5,7},{6,4},{7,5},{8,10},{9,11},{10,... | collective-permute-start | bytes 1572872 | tf_op jit(solution)/shard_map/ppermute | solution.py:226
  153.9 1.2 collective-permute-start.7
  155.1 8.0 %scatter_custom_fusion = s32[2048]{0:T(1024)S(1)} fusion(s32[2048]{0:T(1024)S(1)} %get-tuple-element.36, s32[2048]{0:T(1024)S(1)} %get-tuple-element.37, s32[]{:T(128)} %constant.122.clone.1), kind=kCustom, calls=%fused_computation.41 | custom fusion | bytes 8196 | tf_op jit(solution)/shard_map/scatter | solution.py:280
  163.2 2.4 %lowrank.1 = (bf16[256,512]{1,0:T(8,128)(2,1)}, bf16[256,512]{1,0:T(8,128)(2,1)}) custom-call(f32[64,384]{1,0:T(8,128)} %get-tuple-element.33.g_ref, bf16[512,512]{1,0:T(8,128)(2,1)} %d_ref.5, bf16[64,512]{1,0:T(8,128)(2,1)} %left_ref.3, bf16[64,512]{1,0:T(8,128)(2,1)} %right_ref.3, bf16[64,512]{1,0:T(8,128)(2,1)} %get-tuple-element.27.cin_d_ref, ...), custom_call_target="tpu_custom_call" | custom-call | tf_op jit(solution)/shard_map/lowrank/pallas_call | solution.py:129
  165.6 3.7 %collective-permute-done.5.v1 = bf16[512,512]{1,0:T(8,128)(2,1)S(1)} collective-permute-done((bf16[512,512]{1,0:T(8,128)(2,1)}, bf16[512,512]{1,0:T(8,128)(2,1)S(1)}, u32[]{:S(2)}, u32[]{:S(2)}) %collective-permute-start.5) | collective-permute-done | bytes 524320 | tf_op jit(solution)/shard_map/ppermute | solution.py:226
  169.2 12.4 %collective-permute-done.6.v2 = bf16[512,512]{1,0:T(8,128)(2,1)S(1)} collective-permute-done((bf16[512,512]{1,0:T(8,128)(2,1)}, bf16[512,512]{1,0:T(8,128)(2,1)S(1)}, u32[]{:S(2)}, u32[]{:S(2)}) %collective-permute-start.6) | collective-permute-done | bytes 524320 | tf_op jit(solution)/shard_map/ppermute | solution.py:226
  181.6 0.0 collective-permute-done.7.v3
  181.7 0.8 copy-done.6
  182.4 0.2 copy-done.7
  182.6 0.2 copy-done.2
  182.8 7.2 %finish.1 = (bf16[2048,512]{1,0:T(8,128)(2,1)}, bf16[512,128]{1,0:T(8,128)(2,1)}) custom-call(s32[1]{0:T(128)} %bitcast.x_ref, bf16[512,512]{1,0:T(8,128)(2,1)} %get-tuple-element.19.v0, bf16[512,512]{1,0:T(8,128)(2,1)} %copy-done.5, bf16[512,512]{1,0:T(8,128)(2,1)} %copy-done.6, bf16[512,512]{1,0:T(8,128)(2,1)} %copy-done.7, ...), custom_call_target="tpu_custom_call" | custom-call | tf_op jit(solution)/shard_map/finish/pallas_call | solution.py:212
  190.0 7.8 %all-to-all-start.4 = ((bf16[32,16,128]{2,1,0:T(8,128)(2,1)}), bf16[32,16,128]{2,1,0:T(8,128)(2,1)S(1)}, u32[]{:S(2)}, u32[]{:S(2)}) async-start(bf16[32,16,128]{2,1,0:T(8,128)(2,1)} %bitcast.25), calls=%async_computation.4 | async-start | bytes 262144 | tf_op jit(solution)/shard_map/all_to_all | solution.py:274
  197.8 9.5 %gather_fusion = bf16[2048,512]{1,0:T(8,128)(2,1)S(1)} fusion(bf16[2048,512]{1,0:T(8,128)(2,1)} %get-tuple-element.30, s32[2048]{0:T(1024)S(1)} %fusion.18), kind=kCustom, calls=%fused_computation | custom fusion | bytes 4202496 | tf_op jit(solution)/shard_map/jit(_take)/gather | solution.py:281
  207.3 0.6 broadcast_in_dim.25
  207.9 5.7 %all-to-all-start.5 = ((f32[8,16,128]{2,1,0:T(8,128)}), f32[8,16,128]{2,1,0:T(8,128)S(1)}, u32[]{:S(2)}, u32[]{:S(2)}) async-start(f32[8,16,128]{2,1,0:T(8,128)} %broadcast_in_dim.25), calls=%async_computation.5 | async-start | bytes 131072 | tf_op jit(solution)/shard_map/all_to_all | solution.py:235
  213.6 1.5 broadcast_select_fusion
  215.1 3.3 %all-to-all-done.5 = f32[8,16,128]{2,1,0:T(8,128)S(1)} async-done(((f32[8,16,128]{2,1,0:T(8,128)}), f32[8,16,128]{2,1,0:T(8,128)S(1)}, u32[]{:S(2)}, u32[]{:S(2)}) %all-to-all-start.5) | async-done | bytes 65568 | tf_op jit(solution)/shard_map/all_to_all | solution.py:235
  218.5 0.6 reduce_sum.19
  (35 shorter events, 0.2 us)
Async XLA Ops:
  3.8 60.7 %all-to-all-start = ((bf16[8,64,2048]{2,1,0:T(8,128)(2,1)}), bf16[8,64,2048]{2,1,0:T(8,128)(2,1)S(1)}, u32[]{:S(2)}, u32[]{:S(2)}) async-start(bf16[8,64,2048]{2,1,0:T(8,128)(2,1)} %bitcast.20), calls=%async_computation | async-start | bytes 4194304 | tf_op jit(solution)/shard_map/all_to_all | solution.py:246
  15.3 23.3 %collective-permute-start = (bf16[256,512]{1,0:T(8,128)(2,1)}, bf16[256,512]{1,0:T(8,128)(2,1)S(1)}, u32[]{:S(2)}, u32[]{:S(2)}) collective-permute-start(bf16[256,512]{1,0:T(8,128)(2,1)} %get-tuple-element.17.w0), channel_id=1, source_target_pairs={{0,1},{1,2},{2,3},{3,0},{4,5},{5,6},{6,7},{7,4},{8,9},{9,10},{10,1... | collective-permute-start | bytes 786440 | tf_op jit(solution)/shard_map/ppermute | solution.py:226
  16.5 22.1 %collective-permute-start.1 = (bf16[256,512]{1,0:T(8,128)(2,1)}, bf16[256,512]{1,0:T(8,128)(2,1)S(1)}, u32[]{:S(2)}, u32[]{:S(2)}) collective-permute-start(bf16[256,512]{1,0:T(8,128)(2,1)} %get-tuple-element.17.w0), channel_id=1, source_target_pairs={{0,2},{1,3},{2,0},{3,1},{4,6},{5,7},{6,4},{7,5},{8,10},{9,11},{10,... | collective-permute-start | bytes 786440 | tf_op jit(solution)/shard_map/ppermute | solution.py:226
  19.0 19.7 %collective-permute-start.2 = (bf16[256,512]{1,0:T(8,128)(2,1)}, bf16[256,512]{1,0:T(8,128)(2,1)S(1)}, u32[]{:S(2)}, u32[]{:S(2)}) collective-permute-start(bf16[256,512]{1,0:T(8,128)(2,1)} %get-tuple-element.17.w0), channel_id=1, source_target_pairs={{0,3},{1,0},{2,1},{3,2},{4,7},{5,4},{6,5},{7,6},{8,11},{9,8},{10,9... | collective-permute-start | bytes 786440 | tf_op jit(solution)/shard_map/ppermute | solution.py:226
  20.1 11.6 %collective-permute-start.3 = (f32[64,384]{1,0:T(8,128)}, f32[64,384]{1,0:T(8,128)S(1)}, u32[]{:S(2)}, u32[]{:S(2)}) collective-permute-start(f32[64,384]{1,0:T(8,128)} %get-tuple-element.18), channel_id=1, source_target_pairs={{0,1},{1,0},{2,3},{3,2},{4,5},{5,4},{6,7},{7,6},{8,9},{9,8},{10,11... | collective-permute-start | bytes 294920 | tf_op jit(solution)/shard_map/ppermute | solution.py:230
  32.6 5.4 %collective-permute-start.4 = (f32[64,384]{1,0:T(8,128)S(1)}, f32[64,384]{1,0:T(8,128)S(1)}, u32[]{:S(2)}, u32[]{:S(2)}) collective-permute-start(f32[64,384]{1,0:T(8,128)S(1)} %add.86), channel_id=1, source_target_pairs={{0,2},{1,3},{2,0},{3,1},{4,6},{5,7},{6,4},{7,5},{8,10},{9,11},{10,... | collective-permute-start | bytes 294920 | tf_op jit(solution)/shard_map/ppermute | solution.py:230
  38.6 25.9 %copy-start.8 = (bf16[256,512]{1,0:T(8,128)(2,1)}, bf16[256,512]{1,0:T(8,128)(2,1)S(1)}, u32[]{:S(2)}) copy-start(bf16[256,512]{1,0:T(8,128)(2,1)S(1)} %collective-permute-done.w1) | copy-start | bytes 786436
  38.6 25.9 %copy-start.9 = (bf16[256,512]{1,0:T(8,128)(2,1)}, bf16[256,512]{1,0:T(8,128)(2,1)S(1)}, u32[]{:S(2)}) copy-start(bf16[256,512]{1,0:T(8,128)(2,1)S(1)} %collective-permute-done.1.w2) | copy-start | bytes 786436
  38.6 25.8 %copy-start.10 = (bf16[256,512]{1,0:T(8,128)(2,1)}, bf16[256,512]{1,0:T(8,128)(2,1)S(1)}, u32[]{:S(2)}) copy-start(bf16[256,512]{1,0:T(8,128)(2,1)S(1)} %collective-permute-done.2.w3) | copy-start | bytes 786436
  64.5 1.3 copy-start
  69.8 15.2 %all-to-all-start.1 = ((bf16[8,64,256]{2,1,0:T(8,128)(2,1)}), bf16[8,64,256]{2,1,0:T(8,128)(2,1)S(1)}, u32[]{:S(2)}, u32[]{:S(2)}) async-start(bf16[8,64,256]{2,1,0:T(8,128)(2,1)} %bitcast.24), calls=%async_computation.1 | async-start | bytes 524288 | tf_op jit(solution)/shard_map/all_to_all | solution.py:253
  73.2 18.8 %collective-permute-start.8 = (f32[64,384]{1,0:T(8,128)}, f32[64,384]{1,0:T(8,128)S(1)}, u32[]{:S(2)}, u32[]{:S(2)}) collective-permute-start(f32[64,384]{1,0:T(8,128)} %get-tuple-element.26), channel_id=1, source_target_pairs={{0,4},{4,0},{8,12},{12,8},{16,20},{20,16},{24,28},{28,24},{1,5},{5... | collective-permute-start | bytes 294920 | tf_op jit(solution)/shard_map/ppermute | solution.py:230
  85.0 0.7 copy-start.3
  87.6 54.6 %all-to-all-start.2 = ((bf16[32,64,128]{2,1,0:T(8,128)(2,1)}), bf16[32,64,128]{2,1,0:T(8,128)(2,1)S(1)}, u32[]{:S(2)}, u32[]{:S(2)}) async-start(bf16[32,64,128]{2,1,0:T(8,128)(2,1)} %get-tuple-element.24), calls=%async_computation.2 | async-start | bytes 1048576 | tf_op jit(solution)/shard_map/all_to_all | solution.py:259
  92.0 61.9 %copy-start.15 = (bf16[512,512]{1,0:T(8,128)(2,1)S(1)}, bf16[512,512]{1,0:T(8,128)(2,1)}, u32[]{:S(2)}) copy-start(bf16[512,512]{1,0:T(8,128)(2,1)} %get-tuple-element.22) | copy-start | bytes 1572868
  92.0 63.1 %copy-start.14 = (s32[2048]{0:T(1024)S(1)}, s32[2048]{0:T(1024)}, u32[]{:S(2)}) copy-start(s32[2048]{0:T(1024)} %param.14) | copy-start | bytes 24580
  93.0 15.7 %collective-permute-start.9 = (f32[64,384]{1,0:T(8,128)S(1)}, f32[64,384]{1,0:T(8,128)S(1)}, u32[]{:S(2)}, u32[]{:S(2)}) collective-permute-start(f32[64,384]{1,0:T(8,128)S(1)} %add.95), channel_id=1, source_target_pairs={{0,8},{4,12},{8,0},{12,4},{16,24},{20,28},{24,16},{28,20},{1,9},{5... | collective-permute-start | bytes 294920 | tf_op jit(solution)/shard_map/ppermute | solution.py:230
  108.7 7.5 %collective-permute-start.10 = (f32[64,384]{1,0:T(8,128)S(1)}, f32[64,384]{1,0:T(8,128)S(1)}, u32[]{:S(2)}, u32[]{:S(2)}) collective-permute-start(f32[64,384]{1,0:T(8,128)S(1)} %add.96), channel_id=1, source_target_pairs={{0,16},{4,20},{8,24},{12,28},{16,0},{20,4},{24,8},{28,12},{1,17},{... | collective-permute-start | bytes 294920 | tf_op jit(solution)/shard_map/ppermute | solution.py:230
  117.6 5.3 %collective-permute-start.11 = (bf16[64,640]{1,0:T(8,128)(2,1)S(1)}, bf16[64,640]{1,0:T(8,128)(2,1)S(1)}, u32[]{:S(2)}, u32[]{:S(2)}) collective-permute-start(bf16[64,640]{1,0:T(8,128)(2,1)S(1)} %get-tuple-element.35), channel_id=1, source_target_pairs={{0,32},{32,0},{64,96},{96,64},{128,160},{160,128},{192,224},{224,1... | collective-permute-start | bytes 245768 | tf_op jit(solution)/shard_map/ppermute | solution.py:230
  122.9 11.5 %copy-start.4 = (bf16[2,64,640]{2,1,0:T(8,128)(2,1)}, bf16[2,64,640]{2,1,0:T(8,128)(2,1)S(1)}, u32[]{:S(2)}) copy-start(bf16[2,64,640]{2,1,0:T(8,128)(2,1)S(1)} %pad_maximum_fusion.f0) | copy-start | bytes 491524
  122.9 6.8 %collective-permute-start.12 = (bf16[2,64,640]{2,1,0:T(8,128)(2,1)S(1)}, bf16[2,64,640]{2,1,0:T(8,128)(2,1)S(1)}, u32[]{:S(2)}, u32[]{:S(2)}) collective-permute-start(bf16[2,64,640]{2,1,0:T(8,128)(2,1)S(1)} %pad_maximum_fusion.f0), channel_id=1, source_target_pairs={{0,64},{32,96},{64,128},{96,160},{128,192},{160,224},{192,0},{224,... | collective-permute-start | bytes 491528 | tf_op jit(solution)/shard_map/ppermute | solution.py:226
  124.3 10.1 %collective-permute-start.13 = (bf16[2,64,640]{2,1,0:T(8,128)(2,1)S(1)}, bf16[2,64,640]{2,1,0:T(8,128)(2,1)S(1)}, u32[]{:S(2)}, u32[]{:S(2)}) collective-permute-start(bf16[2,64,640]{2,1,0:T(8,128)(2,1)S(1)} %pad_maximum_fusion.f0), channel_id=1, source_target_pairs={{0,128},{32,160},{64,192},{96,224},{128,0},{160,32},{192,64},{224,... | collective-permute-start | bytes 491528 | tf_op jit(solution)/shard_map/ppermute | solution.py:226
  126.9 7.5 %collective-permute-start.14 = (bf16[2,64,640]{2,1,0:T(8,128)(2,1)S(1)}, bf16[2,64,640]{2,1,0:T(8,128)(2,1)S(1)}, u32[]{:S(2)}, u32[]{:S(2)}) collective-permute-start(bf16[2,64,640]{2,1,0:T(8,128)(2,1)S(1)} %pad_maximum_fusion.f0), channel_id=1, source_target_pairs={{0,192},{32,224},{64,0},{96,32},{128,64},{160,96},{192,128},{224,1... | collective-permute-start | bytes 491528 | tf_op jit(solution)/shard_map/ppermute | solution.py:226
  129.8 4.6 %copy-start.11 = (bf16[2,64,640]{2,1,0:T(8,128)(2,1)}, bf16[2,64,640]{2,1,0:T(8,128)(2,1)S(1)}, u32[]{:S(2)}) copy-start(bf16[2,64,640]{2,1,0:T(8,128)(2,1)S(1)} %collective-permute-done.12.f1) | copy-start | bytes 491524
  134.4 0.7 copy-start.12
  135.0 0.7 copy-start.13
  142.2 39.5 %copy-start.1 = (bf16[32,64,128]{2,1,0:T(8,128)(2,1)}, bf16[32,64,128]{2,1,0:T(8,128)(2,1)S(1)}, u32[]{:S(2)}) copy-start(bf16[32,64,128]{2,1,0:T(8,128)(2,1)S(1)} %all-to-all-done.2) | copy-start | bytes 1572868
  142.2 39.4 %all-to-all-start.3 = ((bf16[32,64,128]{2,1,0:T(8,128)(2,1)}), bf16[32,64,128]{2,1,0:T(8,128)(2,1)S(1)}, u32[]{:S(2)}, u32[]{:S(2)}) async-start(bf16[32,64,128]{2,1,0:T(8,128)(2,1)} %recur.1), calls=%async_computation.3 | async-start | bytes 1048576 | tf_op jit(solution)/shard_map/all_to_all | solution.py:267
  150.0 19.2 %collective-permute-start.5 = (bf16[512,512]{1,0:T(8,128)(2,1)}, bf16[512,512]{1,0:T(8,128)(2,1)S(1)}, u32[]{:S(2)}, u32[]{:S(2)}) collective-permute-start(bf16[512,512]{1,0:T(8,128)(2,1)} %get-tuple-element.20), channel_id=1, source_target_pairs={{0,1},{1,2},{2,3},{3,0},{4,5},{5,6},{6,7},{7,4},{8,9},{9,10},{10,1... | collective-permute-start | bytes 1572872 | tf_op jit(solution)/shard_map/ppermute | solution.py:226
  151.5 30.1 %collective-permute-start.6 = (bf16[512,512]{1,0:T(8,128)(2,1)}, bf16[512,512]{1,0:T(8,128)(2,1)S(1)}, u32[]{:S(2)}, u32[]{:S(2)}) collective-permute-start(bf16[512,512]{1,0:T(8,128)(2,1)} %get-tuple-element.21), channel_id=1, source_target_pairs={{0,2},{1,3},{2,0},{3,1},{4,6},{5,7},{6,4},{7,5},{8,10},{9,11},{10,... | collective-permute-start | bytes 1572872 | tf_op jit(solution)/shard_map/ppermute | solution.py:226
  153.9 27.7 %collective-permute-start.7 = (bf16[512,512]{1,0:T(8,128)(2,1)S(1)}, bf16[512,512]{1,0:T(8,128)(2,1)S(1)}, u32[]{:S(2)}, u32[]{:S(2)}) collective-permute-start(bf16[512,512]{1,0:T(8,128)(2,1)S(1)} %copy-done.15), channel_id=1, source_target_pairs={{0,3},{1,0},{2,1},{3,2},{4,7},{5,4},{6,5},{7,6},{8,11},{9,8},{10,9... | collective-permute-start | bytes 1572872 | tf_op jit(solution)/shard_map/ppermute | solution.py:226
  169.2 12.4 %copy-start.5 = (bf16[512,512]{1,0:T(8,128)(2,1)}, bf16[512,512]{1,0:T(8,128)(2,1)S(1)}, u32[]{:S(2)}) copy-start(bf16[512,512]{1,0:T(8,128)(2,1)S(1)} %collective-permute-done.5.v1) | copy-start | bytes 1572868
  181.6 0.8 copy-start.6
  181.6 1.0 copy-start.7
  181.6 1.1 copy-start.2
  190.0 17.3 %all-to-all-start.4 = ((bf16[32,16,128]{2,1,0:T(8,128)(2,1)}), bf16[32,16,128]{2,1,0:T(8,128)(2,1)S(1)}, u32[]{:S(2)}, u32[]{:S(2)}) async-start(bf16[32,16,128]{2,1,0:T(8,128)(2,1)} %bitcast.25), calls=%async_computation.4 | async-start | bytes 262144 | tf_op jit(solution)/shard_map/all_to_all | solution.py:274
  207.9 10.6 %all-to-all-start.5 = ((f32[8,16,128]{2,1,0:T(8,128)}), f32[8,16,128]{2,1,0:T(8,128)S(1)}, u32[]{:S(2)}, u32[]{:S(2)}) async-start(f32[8,16,128]{2,1,0:T(8,128)} %broadcast_in_dim.25), calls=%async_computation.5 | async-start | bytes 131072 | tf_op jit(solution)/shard_map/all_to_all | solution.py:235
